TPU v7x, 256 devices: a whole 4x4x8 slice. The times are simulated.
256 devices in a mesh: tile: 128 (over z_hi, x, y, core), member: 2 (over z_lo).
Axes of the slice: x: 4, y: 4, z: 8 (z_hi: 4, z_lo: 2; z = z_hi * 2 + z_lo), core: 2. Of those that a mesh axis runs over, the one named last changes fastest.
Arguments:
- fields: bfloat16 [2, 128, 2, 32, 32, 128], P('member', 'tile'), may hold values from -6 to 6
- cotangent: bfloat16 [2, 128, 2, 32, 32, 128], P('member', 'tile'), may hold values from -6 to 6
- edge_map: int32 [128, 4, 2], P('tile'), may hold values from 0 to 3, as said below
- w_first: bfloat16 [3, 3, 128, 128], replicated, may hold values from -0.1875 to 0.1875
- b_first: float32 [128], replicated, may hold values from -3 to 3
- w_second: bfloat16 [3, 3, 128, 128], replicated, may hold values from -0.1875 to 0.1875
- b_second: float32 [128], replicated, may hold values from -3 to 3
Outputs:
- response: bfloat16 [2, 128, 2, 32, 32, 128], P('member', 'tile')
- field_grad: bfloat16 [2, 128, 2, 32, 32, 128], P('member', 'tile')
- first_kernel_grad: float32 [3, 3, 128, 128], replicated
- first_bias_grad: float32 [128], replicated
- second_kernel_grad: float32 [3, 3, 128, 128], replicated
- second_bias_grad: float32 [128], replicated
Inputs may be any that keep to these rules, and one draw needn't show every extreme that they name: Each tile t is its own grid turned by r quarter turns: edge_map[t, g, 0] = (g - r) mod 4, and edge_map[t, g, 1] is 1 exactly when r = 2, or r = 1 and g is even, or r = 3 and g is odd.
All inputs are finite; a program needn't handle non-finite values.
Results may differ from a plain program's by a relative error of at most 0.0065.
Values may be sent and summed in bfloat16 or wider, within the bound.
A program may use at most 64 MiB of HBM per device.

v0:
```python
import jax
import jax.numpy as jnp
from jax import lax
from jax.sharding import PartitionSpec as P

ROW_TILES = 8
ROOT_HALF = 0.7071067811865476
INV_ROOT_TAU = 0.3989422804014327


def shifted(value, axis, steps):
    count = lax.axis_size(axis)
    pairs = [(source, (source + steps) % count) for source in range(count)]
    return lax.ppermute(value, axis, pairs)


def gelu_value(inputs):
    return 0.5 * inputs * (1.0 + jax.scipy.special.erf(inputs * ROOT_HALF))


def gelu_slope(inputs):
    return (
        0.5 * (1.0 + jax.scipy.special.erf(inputs * ROOT_HALF))
        + inputs * jnp.exp(-0.5 * inputs * inputs) * INV_ROOT_TAU
    )


def patches(padded):
    out_rows = padded.shape[-3] - 2
    out_cols = padded.shape[-2] - 2
    pieces = [
        padded[..., row_off : row_off + out_rows, col_off : col_off + out_cols, :]
        for row_off in range(3)
        for col_off in range(3)
    ]
    joined = jnp.concatenate(pieces, axis=-1)
    return joined.reshape(-1, joined.shape[-1])


def rim_strips(tile_data):
    return jnp.stack(
        [
            tile_data[..., 0, :, :],
            tile_data[..., :, -1, :],
            tile_data[..., -1, :, :],
            tile_data[..., :, 0, :],
        ],
        axis=-4,
    )


def orient(strips, chosen_ids, flip_ids):
    shaped_ids = chosen_ids.reshape(chosen_ids.shape + (1, 1, 1))
    shaped_flips = flip_ids.reshape(flip_ids.shape + (1, 1, 1))
    chosen = jnp.zeros_like(strips)
    for candidate in range(4):
        chosen = jnp.where(
            shaped_ids == candidate, jnp.expand_dims(strips[..., candidate, :, :, :], -4), chosen
        )
    flipped = chosen[..., ::-1, :]
    return jnp.where(shaped_flips == 1, flipped, chosen)


def assemble(tile_data, placed):
    top_rim = placed[..., 0, :, :, :]
    right_rim = placed[..., 1, :, :, :]
    bottom_rim = placed[..., 2, :, :, :]
    left_rim = placed[..., 3, :, :, :]
    kind = tile_data.dtype
    top_left = (
        0.5 * (top_rim[..., 0, :].astype(jnp.float32) + left_rim[..., 0, :].astype(jnp.float32))
    ).astype(kind)
    top_right = (
        0.5 * (top_rim[..., -1, :].astype(jnp.float32) + right_rim[..., 0, :].astype(jnp.float32))
    ).astype(kind)
    low_left = (
        0.5 * (bottom_rim[..., 0, :].astype(jnp.float32) + left_rim[..., -1, :].astype(jnp.float32))
    ).astype(kind)
    low_right = (
        0.5
        * (bottom_rim[..., -1, :].astype(jnp.float32) + right_rim[..., -1, :].astype(jnp.float32))
    ).astype(kind)
    top_row = jnp.concatenate([top_left[..., None, :], top_rim, top_right[..., None, :]], axis=-2)
    bottom_row = jnp.concatenate(
        [low_left[..., None, :], bottom_rim, low_right[..., None, :]], axis=-2
    )
    middle = jnp.concatenate(
        [left_rim[..., :, None, :], tile_data, right_rim[..., :, None, :]], axis=-2
    )
    return jnp.concatenate([top_row[..., None, :, :], middle, bottom_row[..., None, :, :]], axis=-3)


def fold_rims(grad_pad):
    interior = grad_pad[..., 1:-1, 1:-1, :]
    top_left = 0.5 * grad_pad[..., 0, 0, :]
    top_right = 0.5 * grad_pad[..., 0, -1, :]
    low_left = 0.5 * grad_pad[..., -1, 0, :]
    low_right = 0.5 * grad_pad[..., -1, -1, :]
    top_rim = grad_pad[..., 0, 1:-1, :].at[..., 0, :].add(top_left).at[..., -1, :].add(top_right)
    right_rim = (
        grad_pad[..., 1:-1, -1, :].at[..., 0, :].add(top_right).at[..., -1, :].add(low_right)
    )
    bottom_rim = (
        grad_pad[..., -1, 1:-1, :].at[..., 0, :].add(low_left).at[..., -1, :].add(low_right)
    )
    left_rim = grad_pad[..., 1:-1, 0, :].at[..., 0, :].add(top_left).at[..., -1, :].add(low_left)
    return (interior, jnp.stack([top_rim, right_rim, bottom_rim, left_rim], axis=-4))


def spread(interior, edge_grads):
    interior = interior.at[..., 0, :, :].add(edge_grads[..., 0, :, :, :])
    interior = interior.at[..., :, -1, :].add(edge_grads[..., 1, :, :, :])
    interior = interior.at[..., -1, :, :].add(edge_grads[..., 2, :, :, :])
    return interior.at[..., :, 0, :].add(edge_grads[..., 3, :, :, :])


def trade_rims(outgoing):
    offsets = (ROW_TILES, -1, -ROW_TILES, 1)
    received = []
    for direction in range(4):
        received.append(shifted(outgoing[(direction + 2) % 4], "tile", offsets[direction]))
    return jnp.stack(received)


def trade_grads(outgoing):
    offsets = (ROW_TILES, -1, -ROW_TILES, 1)
    received = []
    for direction in range(4):
        received.append(
            shifted(
                outgoing[(direction + 2) % 4].astype(jnp.bfloat16), "tile", offsets[direction]
            ).astype(jnp.float32)
        )
    return jnp.stack(received)


def pad_tile(tile_data, tables):
    side_ids, flip_marks, inverse, inverse_marks = tables
    outgoing = orient(rim_strips(tile_data), side_ids, flip_marks)
    incoming = trade_rims(outgoing)
    return assemble(tile_data, orient(incoming, inverse, inverse_marks))


def unpad_tile(grad_pad, tables):
    side_ids, flip_marks, inverse, inverse_marks = tables
    interior, placed = fold_rims(grad_pad)
    outgoing = orient(placed, side_ids, flip_marks)
    incoming = trade_grads(outgoing)
    return spread(interior, orient(incoming, inverse, inverse_marks))


def apply_cat(padded, weights_cat, out_rows, out_cols):
    product = jnp.dot(patches(padded), weights_cat, preferred_element_type=jnp.float32)
    return product.reshape(padded.shape[0], out_rows, out_cols, -1)


def forward_conv(tile_data, weights_cat, tables):
    tile_side = tile_data.shape[1]
    padded = pad_tile(tile_data, tables)
    result = apply_cat(padded, weights_cat, tile_side, tile_side)
    return (result, padded)


def back_conv(grad_data, weights_flip):
    tile_side = grad_data.shape[1]
    zero_pad = jnp.pad(grad_data, ((0, 0), (2, 2), (2, 2), (0, 0)))
    return apply_cat(zero_pad, weights_flip, tile_side + 2, tile_side + 2)


def kernel_term(padded, grad_data):
    channels = grad_data.shape[-1]
    total = lax.dot_general(
        patches(padded),
        grad_data.reshape(-1, channels),
        (((0,), (0,)), ((), ())),
        preferred_element_type=jnp.float32,
    )
    return total.reshape(3, 3, channels, channels)


def per_device(fields, cotangent, edge_map, w_first, b_first, w_second, b_second):
    frames, tile_side, channels = (fields.shape[2], fields.shape[3], fields.shape[5])
    source = fields.reshape(fields.shape[2:])
    upstream = cotangent.reshape(cotangent.shape[2:])
    side_ids = edge_map[0, :, 0]
    flip_marks = edge_map[0, :, 1]
    directions = jnp.arange(4, dtype=jnp.int32)
    inverse = jnp.sum(directions[None, :] * (side_ids[None, :] == directions[:, None]), axis=1)
    inverse_marks = jnp.take(flip_marks, inverse)
    tables = (side_ids, flip_marks, inverse, inverse_marks)
    first_cat = w_first.reshape(9 * channels, channels)
    second_cat = w_second.reshape(9 * channels, channels)
    first_flip = w_first[::-1, ::-1].transpose(0, 1, 3, 2).reshape(9 * channels, channels)
    second_flip = w_second[::-1, ::-1].transpose(0, 1, 3, 2).reshape(9 * channels, channels)
    norm_scale = float(
        lax.axis_size("tile") * lax.axis_size("member") * frames * tile_side * tile_side
    ) ** (-0.5)
    pre_one, pad_first = forward_conv(source, first_cat, tables)
    hidden_one = pre_one + b_first
    activity = gelu_value(hidden_one).astype(jnp.bfloat16)
    pre_two, pad_second = forward_conv(activity, second_cat, tables)
    hidden_two = pre_two + b_second
    response = gelu_value(hidden_two).astype(jnp.bfloat16)
    grad_second = (upstream.astype(jnp.float32) * gelu_slope(hidden_two)).astype(jnp.bfloat16)
    kernel_two = kernel_term(pad_second, grad_second)
    bias_two = jnp.sum(grad_second.astype(jnp.float32), axis=(0, 1, 2))
    grad_act = unpad_tile(back_conv(grad_second, second_flip), tables)
    grad_first = (grad_act * gelu_slope(hidden_one)).astype(jnp.bfloat16)
    kernel_one = kernel_term(pad_first, grad_first)
    bias_one = jnp.sum(grad_first.astype(jnp.float32), axis=(0, 1, 2))
    field_grad = unpad_tile(back_conv(grad_first, first_flip), tables).astype(jnp.bfloat16)
    kernel_one, bias_one, kernel_two, bias_two = lax.psum(
        (kernel_one, bias_one, kernel_two, bias_two), ("tile", "member")
    )
    return (
        response.reshape(fields.shape),
        field_grad.reshape(fields.shape),
        kernel_one * norm_scale,
        bias_one * norm_scale,
        kernel_two * norm_scale,
        bias_two * norm_scale,
    )


def solution(mesh):
    in_specs = (
        P("member", "tile", None, None, None, None),
        P("member", "tile", None, None, None, None),
        P("tile", None, None),
        P(),
        P(),
        P(),
        P(),
    )
    out_specs = (
        P("member", "tile", None, None, None, None),
        P("member", "tile", None, None, None, None),
        P(),
        P(),
        P(),
        P(),
    )
    return jax.shard_map(
        per_device, mesh=mesh, in_specs=in_specs, out_specs=out_specs, check_vma=False
    )
```

profile of v0, /device:TPU:2, one launch (start us, length us, event | category | flops | bytes accessed | tf_op | source)
XLA Modules:
  0.0 479.1 jit_solution(9307611065890658141)
XLA Ops:
  7.2 0.8 slice_bitcast_fusion.27
  8.0 1.0 fusion.81
  10.2 1.6 collective-permute-start.3
  11.8 3.5 collective-permute-start.2
  15.3 6.0 %collective-permute-start.1 = (bf16[2,32,128]{2,1,0:T(8,128)(2,1)S(1)}, bf16[2,32,128]{2,1,0:T(8,128)(2,1)S(1)}, u32[]{:S(2)}, u32[]{:S(2)}) collective-permute-start(bf16[2,32,128]{2,1,0:T(8,128)(2,1)S(1)} %get-tuple-element.401), channel_id=1, source_target_pairs={{0,240},{2,242},{4,244},{6,246},{8,248},{10,250},{12,252},{14,254}... | collective-permute-start | bytes 49160 | tf_op jit(solution)/shard_map/ppermute | solution.py:14
  22.9 1.2 copy.158
  24.8 1.2 copy.140
  27.7 1.1 fusion.79
  29.2 1.1 constant_dynamic-update-slice_fusion.5
  30.4 1.1 constant_dynamic-update-slice_fusion.3
  31.5 1.5 fusion.78
  33.5 1.4 fusion.84
  36.3 3.8 collective-permute-start.6
  40.0 6.2 %collective-permute-start.5 = (bf16[2,32,128]{2,1,0:T(8,128)(2,1)S(1)}, bf16[2,32,128]{2,1,0:T(8,128)(2,1)S(1)}, u32[]{:S(2)}, u32[]{:S(2)}) collective-permute-start(bf16[2,32,128]{2,1,0:T(8,128)(2,1)S(1)} %get-tuple-element.391), channel_id=1, source_target_pairs={{0,240},{2,242},{4,244},{6,246},{8,248},{10,250},{12,252},{14,254}... | collective-permute-start | bytes 49160 | tf_op jit(solution)/shard_map/ppermute | solution.py:14
  46.2 1.9 constant_dynamic-update-slice_fusion.18
  48.2 0.9 constant_dynamic-update-slice_fusion.17
  49.1 0.9 constant_dynamic-update-slice_fusion.16
  50.0 1.9 constant_dynamic-update-slice_fusion.15
  51.9 0.9 constant_dynamic-update-slice_fusion.14
  52.8 0.9 constant_dynamic-update-slice_fusion.13
  53.6 0.9 constant_dynamic-update-slice_fusion.12
  54.5 0.9 constant_dynamic-update-slice_fusion.11
  55.5 0.9 constant_dynamic-update-slice_fusion.10
  56.3 6.7 %copy.180 = bf16[1152,2048]{1,0:T(8,128)(2,1)} copy(bf16[1152,2048]{0,1:T(8,128)(2,1)} %bitcast.102) | data formatting | bytes 9437184 | tf_op jit(solution)/shard_map/dot_general | solution.py:172
  64.6 0.8 constant_dynamic-update-slice_fusion.9
  66.4 4.8 %copy.182 = bf16[2,32,32,1152]{3,2,1,0:T(8,128)(2,1)} copy(bf16[2,32,32,1152]{3,1,0,2:T(8,128)(2,1)S(1)} %slice_dynamic-update-slice_fusion) | data formatting | bytes 9437184 | tf_op jit(solution)/shard_map/concatenate | solution.py:36
  71.3 2.5 convert_reduce_fusion
  76.5 2.3 fusion.2
  80.7 6.7 %copy.183 = bf16[1152,2048]{1,0:T(8,128)(2,1)} copy(bf16[1152,2048]{0,1:T(8,128)(2,1)} %bitcast.263) | data formatting | bytes 9437184 | tf_op jit(solution)/shard_map/dot_general | solution.py:172
  88.2 0.8 copy.260
  93.7 1.4 select_select_fusion.3
  95.1 0.9 rev.35
  96.0 0.9 select_convert_fusion.1
  97.1 3.8 collective-permute-start.10
  100.8 6.0 %collective-permute-start.9 = (bf16[2,32,128]{2,1,0:T(8,128)(2,1)S(1)}, bf16[2,32,128]{2,1,0:T(8,128)(2,1)S(1)}, u32[]{:S(2)}, u32[]{:S(2)}) collective-permute-start(bf16[2,32,128]{2,1,0:T(8,128)(2,1)S(1)} %get-tuple-element.381), channel_id=1, source_target_pairs={{0,240},{2,242},{4,244},{6,246},{8,248},{10,250},{12,252},{14,254}... | collective-permute-start | bytes 49160 | tf_op jit(solution)/shard_map/ppermute | solution.py:14
  106.9 4.6 fusion.86
  111.6 1.1 copy.185
  113.8 0.9 convert_reduce_fusion.1
  117.4 2.1 fusion
  119.7 73.3 %all-reduce.2 = (f32[128]{0:T(128)S(1)}, f32[128]{0:T(128)S(1)}) all-reduce(f32[128]{0:T(128)S(1)} %get-tuple-element.318, f32[128]{0:T(128)S(1)} %copy-done.40), channel_id=1, replica_groups=mesh['tile'=128,'member'=2] {'tile','member'}, use_global_device_ids=true, to_apply=%region_3.4 | all-reduce | flops 256 | bytes 2048 | tf_op jit(solution)/shard_map/psum | solution.py:212
  194.1 2.3 collective-permute-start.15
  196.4 3.5 collective-permute-start.14
  199.9 5.4 %collective-permute-start.13 = (bf16[2,32,128]{2,1,0:T(8,128)(2,1)S(1)}, bf16[2,32,128]{2,1,0:T(8,128)(2,1)S(1)}, u32[]{:S(2)}, u32[]{:S(2)}) collective-permute-start(bf16[2,32,128]{2,1,0:T(8,128)(2,1)S(1)} %get-tuple-element.377), channel_id=1, source_target_pairs={{0,240},{2,242},{4,244},{6,246},{8,248},{10,250},{12,252},{14,254}... | collective-permute-start | bytes 49160 | tf_op jit(solution)/shard_map/ppermute | solution.py:14
  205.3 4.5 fusion.85
  211.7 1.1 copy.186
  212.8 255.2 %all-reduce.6.cloned.1.call-done = (f32[3,3,128,128]{3,2,1,0:T(8,128)}, f32[3,3,128,128]{3,2,1,0:T(8,128)}) async-done(((f32[3,3,128,128]{3,2,1,0:T(8,128)}, f32[3,3,128,128]{3,2,1,0:T(8,128)}), (f32[3,3,128,128]{3,2,1,0:T(8,128)}, f32[3,3,128,128]{3,2,1,0:T(8,128)})) %all-reduce.6.cloned.1.call-update) | async-done | bytes 1179664 | tf_op jit(solution)/shard_map/psum | solution.py:212
  468.0 1.9 broadcast_multiply_fusion.1
  469.9 1.9 broadcast_multiply_fusion
  (257 shorter events, 26.2 us)
Async XLA Ops:
  7.2 20.0 %copy-start = (bf16[1,1,2,32,32,128]{5,4,3,2,1,0:T(8,128)(2,1)S(1)}, bf16[1,1,2,32,32,128]{5,4,3,2,1,0:T(8,128)(2,1)}, u32[]{:S(2)}) copy-start(bf16[1,1,2,32,32,128]{5,4,3,2,1,0:T(8,128)(2,1)} %param.55) | copy-start | bytes 1572868
  7.2 460.8 %all-reduce.6.cloned.1.call-start = ((), (), s32[]{:S(2)}) async-start(), calls=%async_computation | async-start | bytes 2359296 | tf_op jit(solution)/shard_map/psum | solution.py:212
  9.8 26.1 %copy-start.22 = (pred[4]{0:T(512)(128)(4,1)}, pred[4]{0:T(512)(128)(4,1)S(1)}, u32[]{:S(2)}) copy-start(pred[4]{0:T(512)(128)(4,1)S(1)} %get-tuple-element.427) | copy-start | bytes 16
  9.8 26.1 %copy-start.24 = (pred[4]{0:T(512)(128)(4,1)}, pred[4]{0:T(512)(128)(4,1)S(1)}, u32[]{:S(2)}) copy-start(pred[4]{0:T(512)(128)(4,1)S(1)} %get-tuple-element.428) | copy-start | bytes 16
  9.8 26.1 %copy-start.26 = (pred[4]{0:T(512)(128)(4,1)}, pred[4]{0:T(512)(128)(4,1)S(1)}, u32[]{:S(2)}) copy-start(pred[4]{0:T(512)(128)(4,1)S(1)} %get-tuple-element.429) | copy-start | bytes 16
  9.8 26.1 %copy-start.28 = (pred[4]{0:T(512)(128)(4,1)}, pred[4]{0:T(512)(128)(4,1)S(1)}, u32[]{:S(2)}) copy-start(pred[4]{0:T(512)(128)(4,1)S(1)} %get-tuple-element.430) | copy-start | bytes 16
  9.8 26.1 %copy-start.32 = (pred[4]{0:T(512)(128)(4,1)}, pred[4]{0:T(512)(128)(4,1)S(1)}, u32[]{:S(2)}) copy-start(pred[4]{0:T(512)(128)(4,1)S(1)} %get-tuple-element.426) | copy-start | bytes 16
  10.1 16.6 %collective-permute-start = (bf16[2,32,128]{2,1,0:T(8,128)(2,1)S(1)}, bf16[2,32,128]{2,1,0:T(8,128)(2,1)S(1)}, u32[]{:S(2)}, u32[]{:S(2)}) collective-permute-start(bf16[2,32,128]{2,1,0:T(8,128)(2,1)S(1)} %get-tuple-element.398), channel_id=1, source_target_pairs={{0,2},{2,4},{4,6},{6,8},{8,10},{10,12},{12,14},{14,16},{16,18},{18... | collective-permute-start | bytes 49160 | tf_op jit(solution)/shard_map/ppermute | solution.py:14
  10.2 16.5 %collective-permute-start.3 = (bf16[2,32,128]{2,1,0:T(8,128)(2,1)S(1)}, bf16[2,32,128]{2,1,0:T(8,128)(2,1)S(1)}, u32[]{:S(2)}, u32[]{:S(2)}) collective-permute-start(bf16[2,32,128]{2,1,0:T(8,128)(2,1)S(1)} %get-tuple-element.399), channel_id=1, source_target_pairs={{0,16},{2,18},{4,20},{6,22},{8,24},{10,26},{12,28},{14,30},{16,32}... | collective-permute-start | bytes 49160 | tf_op jit(solution)/shard_map/ppermute | solution.py:14
  11.8 15.0 %collective-permute-start.2 = (bf16[2,32,128]{2,1,0:T(8,128)(2,1)S(1)}, bf16[2,32,128]{2,1,0:T(8,128)(2,1)S(1)}, u32[]{:S(2)}, u32[]{:S(2)}) collective-permute-start(bf16[2,32,128]{2,1,0:T(8,128)(2,1)S(1)} %get-tuple-element.400), channel_id=1, source_target_pairs={{0,254},{2,0},{4,2},{6,4},{8,6},{10,8},{12,10},{14,12},{16,14},{18... | collective-permute-start | bytes 49160 | tf_op jit(solution)/shard_map/ppermute | solution.py:14
  15.3 11.5 %collective-permute-start.1 = (bf16[2,32,128]{2,1,0:T(8,128)(2,1)S(1)}, bf16[2,32,128]{2,1,0:T(8,128)(2,1)S(1)}, u32[]{:S(2)}, u32[]{:S(2)}) collective-permute-start(bf16[2,32,128]{2,1,0:T(8,128)(2,1)S(1)} %get-tuple-element.401), channel_id=1, source_target_pairs={{0,240},{2,242},{4,244},{6,246},{8,248},{10,250},{12,252},{14,254}... | collective-permute-start | bytes 49160 | tf_op jit(solution)/shard_map/ppermute | solution.py:14
  22.8 40.4 %copy-start.14 = (pred[4]{0:T(512)(128)(4,1)}, pred[4]{0:T(512)(128)(4,1)S(1)}, u32[]{:S(2)}) copy-start(pred[4]{0:T(512)(128)(4,1)S(1)} %get-tuple-element.432) | copy-start | bytes 16
  22.8 40.4 %copy-start.16 = (pred[4]{0:T(512)(128)(4,1)}, pred[4]{0:T(512)(128)(4,1)S(1)}, u32[]{:S(2)}) copy-start(pred[4]{0:T(512)(128)(4,1)S(1)} %get-tuple-element.433) | copy-start | bytes 16
  22.9 40.4 %copy-start.18 = (pred[4]{0:T(512)(128)(4,1)}, pred[4]{0:T(512)(128)(4,1)S(1)}, u32[]{:S(2)}) copy-start(pred[4]{0:T(512)(128)(4,1)S(1)} %get-tuple-element.434) | copy-start | bytes 16
  22.9 40.4 %copy-start.20 = (pred[4]{0:T(512)(128)(4,1)}, pred[4]{0:T(512)(128)(4,1)S(1)}, u32[]{:S(2)}) copy-start(pred[4]{0:T(512)(128)(4,1)S(1)} %get-tuple-element.435) | copy-start | bytes 16
  22.9 40.4 %copy-start.30 = (pred[4]{0:T(512)(128)(4,1)}, pred[4]{0:T(512)(128)(4,1)S(1)}, u32[]{:S(2)}) copy-start(pred[4]{0:T(512)(128)(4,1)S(1)} %get-tuple-element.431) | copy-start | bytes 16
  29.2 4.3 copy-start.5
  36.0 16.8 %copy-start.2 = (bf16[2,32,32,128]{3,2,1,0:T(8,128)(2,1)S(1)}, bf16[2,32,32,128]{3,2,1,0:T(8,128)(2,1)}, u32[]{:S(2)}) copy-start(bf16[2,32,32,128]{3,2,1,0:T(8,128)(2,1)} %get-tuple-element.321) | copy-start | bytes 1572868
  36.0 17.7 %copy-start.4 = (bf16[2,32,32,128]{3,2,1,0:T(8,128)(2,1)S(1)}, bf16[2,32,32,128]{3,2,1,0:T(8,128)(2,1)}, u32[]{:S(2)}) copy-start(bf16[2,32,32,128]{3,2,1,0:T(8,128)(2,1)} %get-tuple-element.353) | copy-start | bytes 1572868
  36.0 18.5 %copy-start.3 = (bf16[2,32,32,128]{3,2,1,0:T(8,128)(2,1)S(1)}, bf16[2,32,32,128]{3,2,1,0:T(8,128)(2,1)}, u32[]{:S(2)}) copy-start(bf16[2,32,32,128]{3,2,1,0:T(8,128)(2,1)} %get-tuple-element.352) | copy-start | bytes 1572868
  36.0 19.5 %copy-start.1 = (bf16[2,32,32,128]{3,2,1,0:T(8,128)(2,1)S(1)}, bf16[2,32,32,128]{3,2,1,0:T(8,128)(2,1)}, u32[]{:S(2)}) copy-start(bf16[2,32,32,128]{3,2,1,0:T(8,128)(2,1)} %get-tuple-element.350) | copy-start | bytes 1572868
  36.1 27.0 %collective-permute-start.4 = (bf16[2,32,128]{2,1,0:T(8,128)(2,1)S(1)}, bf16[2,32,128]{2,1,0:T(8,128)(2,1)S(1)}, u32[]{:S(2)}, u32[]{:S(2)}) collective-permute-start(bf16[2,32,128]{2,1,0:T(8,128)(2,1)S(1)} %get-tuple-element.388), channel_id=1, source_target_pairs={{0,2},{2,4},{4,6},{6,8},{8,10},{10,12},{12,14},{14,16},{16,18},{18... | collective-permute-start | bytes 49160 | tf_op jit(solution)/shard_map/ppermute | solution.py:14
  36.2 26.9 %collective-permute-start.7 = (bf16[2,32,128]{2,1,0:T(8,128)(2,1)S(1)}, bf16[2,32,128]{2,1,0:T(8,128)(2,1)S(1)}, u32[]{:S(2)}, u32[]{:S(2)}) collective-permute-start(bf16[2,32,128]{2,1,0:T(8,128)(2,1)S(1)} %get-tuple-element.389), channel_id=1, source_target_pairs={{0,16},{2,18},{4,20},{6,22},{8,24},{10,26},{12,28},{14,30},{16,32}... | collective-permute-start | bytes 49160 | tf_op jit(solution)/shard_map/ppermute | solution.py:14
  36.3 26.8 %collective-permute-start.6 = (bf16[2,32,128]{2,1,0:T(8,128)(2,1)S(1)}, bf16[2,32,128]{2,1,0:T(8,128)(2,1)S(1)}, u32[]{:S(2)}, u32[]{:S(2)}) collective-permute-start(bf16[2,32,128]{2,1,0:T(8,128)(2,1)S(1)} %get-tuple-element.390), channel_id=1, source_target_pairs={{0,254},{2,0},{4,2},{6,4},{8,6},{10,8},{12,10},{14,12},{16,14},{18... | collective-permute-start | bytes 49160 | tf_op jit(solution)/shard_map/ppermute | solution.py:14
  40.0 23.0 %collective-permute-start.5 = (bf16[2,32,128]{2,1,0:T(8,128)(2,1)S(1)}, bf16[2,32,128]{2,1,0:T(8,128)(2,1)S(1)}, u32[]{:S(2)}, u32[]{:S(2)}) collective-permute-start(bf16[2,32,128]{2,1,0:T(8,128)(2,1)S(1)} %get-tuple-element.391), channel_id=1, source_target_pairs={{0,240},{2,242},{4,244},{6,246},{8,248},{10,250},{12,252},{14,254}... | collective-permute-start | bytes 49160 | tf_op jit(solution)/shard_map/ppermute | solution.py:14
  66.4 4.9 %copy-start.6 = (bf16[3,3,128,128]{3,2,1,0:T(8,128)(2,1)S(1)}, bf16[3,3,128,128]{3,2,1,0:T(8,128)(2,1)}, u32[]{:S(2)}) copy-start(bf16[3,3,128,128]{3,2,1,0:T(8,128)(2,1)} %param.60) | copy-start | bytes 884740
  66.4 4.9 %copy-start.38 = (bf16[1,1,2,32,32,128]{5,4,3,2,1,0:T(8,128)(2,1)S(1)}, bf16[1,1,2,32,32,128]{5,4,3,2,1,0:T(8,128)(2,1)}, u32[]{:S(2)}) copy-start(bf16[1,1,2,32,32,128]{5,4,3,2,1,0:T(8,128)(2,1)} %param.56) | copy-start | bytes 1572868
  66.4 4.9 %copy-start.39 = (f32[128]{0:T(128)S(1)}, f32[128]{0:T(128)}, u32[]{:S(2)}) copy-start(f32[128]{0:T(128)} %param.61) | copy-start | bytes 1540
  96.9 15.9 %collective-permute-start.8 = (bf16[2,32,128]{2,1,0:T(8,128)(2,1)S(1)}, bf16[2,32,128]{2,1,0:T(8,128)(2,1)S(1)}, u32[]{:S(2)}, u32[]{:S(2)}) collective-permute-start(bf16[2,32,128]{2,1,0:T(8,128)(2,1)S(1)} %get-tuple-element.378), channel_id=1, source_target_pairs={{0,2},{2,4},{4,6},{6,8},{8,10},{10,12},{12,14},{14,16},{16,18},{18... | collective-permute-start | bytes 49160 | tf_op jit(solution)/shard_map/ppermute | solution.py:14
  97.0 15.8 %collective-permute-start.11 = (bf16[2,32,128]{2,1,0:T(8,128)(2,1)S(1)}, bf16[2,32,128]{2,1,0:T(8,128)(2,1)S(1)}, u32[]{:S(2)}, u32[]{:S(2)}) collective-permute-start(bf16[2,32,128]{2,1,0:T(8,128)(2,1)S(1)} %get-tuple-element.379), channel_id=1, source_target_pairs={{0,16},{2,18},{4,20},{6,22},{8,24},{10,26},{12,28},{14,30},{16,32}... | collective-permute-start | bytes 49160 | tf_op jit(solution)/shard_map/ppermute | solution.py:14
  97.1 15.8 %collective-permute-start.10 = (bf16[2,32,128]{2,1,0:T(8,128)(2,1)S(1)}, bf16[2,32,128]{2,1,0:T(8,128)(2,1)S(1)}, u32[]{:S(2)}, u32[]{:S(2)}) collective-permute-start(bf16[2,32,128]{2,1,0:T(8,128)(2,1)S(1)} %get-tuple-element.380), channel_id=1, source_target_pairs={{0,254},{2,0},{4,2},{6,4},{8,6},{10,8},{12,10},{14,12},{16,14},{18... | collective-permute-start | bytes 49160 | tf_op jit(solution)/shard_map/ppermute | solution.py:14
  100.8 12.0 %collective-permute-start.9 = (bf16[2,32,128]{2,1,0:T(8,128)(2,1)S(1)}, bf16[2,32,128]{2,1,0:T(8,128)(2,1)S(1)}, u32[]{:S(2)}, u32[]{:S(2)}) collective-permute-start(bf16[2,32,128]{2,1,0:T(8,128)(2,1)S(1)} %get-tuple-element.381), channel_id=1, source_target_pairs={{0,240},{2,242},{4,244},{6,246},{8,248},{10,250},{12,252},{14,254}... | collective-permute-start | bytes 49160 | tf_op jit(solution)/shard_map/ppermute | solution.py:14
  106.8 6.1 %copy-start.15 = (pred[4]{0:T(512)(128)(4,1)S(1)}, pred[4]{0:T(512)(128)(4,1)}, u32[]{:S(2)}) copy-start(pred[4]{0:T(512)(128)(4,1)} %copy-done.14) | copy-start | bytes 16
  106.8 6.1 %copy-start.17 = (pred[4]{0:T(512)(128)(4,1)S(1)}, pred[4]{0:T(512)(128)(4,1)}, u32[]{:S(2)}) copy-start(pred[4]{0:T(512)(128)(4,1)} %copy-done.16) | copy-start | bytes 16
  106.8 6.1 %copy-start.19 = (pred[4]{0:T(512)(128)(4,1)S(1)}, pred[4]{0:T(512)(128)(4,1)}, u32[]{:S(2)}) copy-start(pred[4]{0:T(512)(128)(4,1)} %copy-done.18) | copy-start | bytes 16
  106.8 6.1 %copy-start.21 = (pred[4]{0:T(512)(128)(4,1)S(1)}, pred[4]{0:T(512)(128)(4,1)}, u32[]{:S(2)}) copy-start(pred[4]{0:T(512)(128)(4,1)} %copy-done.20) | copy-start | bytes 16
  106.8 6.2 %copy-start.31 = (pred[4]{0:T(512)(128)(4,1)S(1)}, pred[4]{0:T(512)(128)(4,1)}, u32[]{:S(2)}) copy-start(pred[4]{0:T(512)(128)(4,1)} %copy-done.30) | copy-start | bytes 16
  111.4 2.3 copy-start.37
  117.4 76.2 %copy-start.35 = (f32[2,1,1,128]{3,1,2,0:T(1,128)S(1)}, f32[2,1,1,128]{3,1,2,0:T(1,128)}, u32[]{:S(2)}) copy-start(f32[2,1,1,128]{3,1,2,0:T(1,128)} %copy-done.34) | copy-start | bytes 3076
  117.4 76.3 %copy-start.23 = (pred[4]{0:T(512)(128)(4,1)S(1)}, pred[4]{0:T(512)(128)(4,1)}, u32[]{:S(2)}) copy-start(pred[4]{0:T(512)(128)(4,1)} %copy-done.22) | copy-start | bytes 16
  117.4 76.3 %copy-start.25 = (pred[4]{0:T(512)(128)(4,1)S(1)}, pred[4]{0:T(512)(128)(4,1)}, u32[]{:S(2)}) copy-start(pred[4]{0:T(512)(128)(4,1)} %copy-done.24) | copy-start | bytes 16
  117.4 76.3 %copy-start.27 = (pred[4]{0:T(512)(128)(4,1)S(1)}, pred[4]{0:T(512)(128)(4,1)}, u32[]{:S(2)}) copy-start(pred[4]{0:T(512)(128)(4,1)} %copy-done.26) | copy-start | bytes 16
  117.4 76.3 %copy-start.29 = (pred[4]{0:T(512)(128)(4,1)S(1)}, pred[4]{0:T(512)(128)(4,1)}, u32[]{:S(2)}) copy-start(pred[4]{0:T(512)(128)(4,1)} %copy-done.28) | copy-start | bytes 16
  117.4 76.5 %copy-start.33 = (pred[4]{0:T(512)(128)(4,1)S(1)}, pred[4]{0:T(512)(128)(4,1)}, u32[]{:S(2)}) copy-start(pred[4]{0:T(512)(128)(4,1)} %copy-done.32) | copy-start | bytes 16
  194.0 16.6 %collective-permute-start.12 = (bf16[2,32,128]{2,1,0:T(8,128)(2,1)S(1)}, bf16[2,32,128]{2,1,0:T(8,128)(2,1)S(1)}, u32[]{:S(2)}, u32[]{:S(2)}) collective-permute-start(bf16[2,32,128]{2,1,0:T(8,128)(2,1)S(1)} %get-tuple-element.374), channel_id=1, source_target_pairs={{0,2},{2,4},{4,6},{6,8},{8,10},{10,12},{12,14},{14,16},{16,18},{18... | collective-permute-start | bytes 49160 | tf_op jit(solution)/shard_map/ppermute | solution.py:14
  194.1 16.6 %collective-permute-start.15 = (bf16[2,32,128]{2,1,0:T(8,128)(2,1)S(1)}, bf16[2,32,128]{2,1,0:T(8,128)(2,1)S(1)}, u32[]{:S(2)}, u32[]{:S(2)}) collective-permute-start(bf16[2,32,128]{2,1,0:T(8,128)(2,1)S(1)} %get-tuple-element.375), channel_id=1, source_target_pairs={{0,16},{2,18},{4,20},{6,22},{8,24},{10,26},{12,28},{14,30},{16,32}... | collective-permute-start | bytes 49160 | tf_op jit(solution)/shard_map/ppermute | solution.py:14
  196.4 14.3 %collective-permute-start.14 = (bf16[2,32,128]{2,1,0:T(8,128)(2,1)S(1)}, bf16[2,32,128]{2,1,0:T(8,128)(2,1)S(1)}, u32[]{:S(2)}, u32[]{:S(2)}) collective-permute-start(bf16[2,32,128]{2,1,0:T(8,128)(2,1)S(1)} %get-tuple-element.376), channel_id=1, source_target_pairs={{0,254},{2,0},{4,2},{6,4},{8,6},{10,8},{12,10},{14,12},{16,14},{18... | collective-permute-start | bytes 49160 | tf_op jit(solution)/shard_map/ppermute | solution.py:14
  199.9 10.8 %collective-permute-start.13 = (bf16[2,32,128]{2,1,0:T(8,128)(2,1)S(1)}, bf16[2,32,128]{2,1,0:T(8,128)(2,1)S(1)}, u32[]{:S(2)}, u32[]{:S(2)}) collective-permute-start(bf16[2,32,128]{2,1,0:T(8,128)(2,1)S(1)} %get-tuple-element.377), channel_id=1, source_target_pairs={{0,240},{2,242},{4,244},{6,246},{8,248},{10,250},{12,252},{14,254}... | collective-permute-start | bytes 49160 | tf_op jit(solution)/shard_map/ppermute | solution.py:14
  (10 other events, 15.0 us)
Sparse Core Ops, SparseCore 0:
  210.8 257.1 all-reduce.5
where the time goes:
time: 489 us; the launch traced here: 479 us
  waiting for transfers between devices  255 us (52%)
  blocking collectives  73.3 us (15%)
  local copies, waits for them, and re-layouts  56.4 us (12%)
  starting transfers between devices  42.5 us (9%)
  other arithmetic  18.3 us (4%)
  matrix products  17.4 us (4%)
  between operations  15.9 us (3%)
    psum x1, waiting for transfers between devices, per_device(): lax.psum((kernel_one, bias_one, kernel_two, bias_two), ('tile', 'member'))  255 us
    psum x1, blocking collectives, per_device(): lax.psum((kernel_one, bias_one, kernel_two, bias_two), ('tile', 'member'))  73.3 us
    ppermute x16, starting transfers between devices, shifted(): return lax.ppermute(value, axis, pairs)  42.5 us
    unnamed x134, local copies, waits for them, and re-layouts  23.3 us
    dot_general x2, local copies, waits for them, and re-layouts, kernel_term(): lax.dot_general(patches(padded), grad_data.reshape(-1, channels), (((0,),...  13.4 us
  transfers between devices with their start and end apart: 17, of which 1 were waited for; matrix products, arithmetic and copies ran while one was open for 7% of the time, Pallas kernels for 0%

commit v1 on v0

--- a/solution.py
+++ b/solution.py
@@ -210,7 +210,7 @@
     bias_one = jnp.sum(grad_first.astype(jnp.float32), axis=(0, 1, 2))
     field_grad = unpad_tile(back_conv(grad_first, first_flip), tables).astype(jnp.bfloat16)
     kernel_one, bias_one, kernel_two, bias_two = lax.psum(
-        (kernel_one, bias_one, kernel_two, bias_two), ("tile", "member")
+        lax.psum((kernel_one, bias_one, kernel_two, bias_two), "member"), "tile"
     )
     return (
         response.reshape(fields.shape),

time: 489 us -> 1780 us (3.64); the launches traced: 479 us -> 1750 us
  waiting for transfers between devices: 255 us -> 1280 us
  blocking collectives: 73.3 us -> 320 us
    psum x1 -> x2, waiting for transfers between devices: 255 us -> 1280 us  [the longest x1 1280 us: per_device(): lax.psum(lax.psum((kernel_one, bias_one, kernel_two, bias_two), 'member')...]
    psum x1 -> x2, blocking collectives: 73.3 us -> 320 us  [the longest x1 315 us: per_device(): lax.psum(lax.psum((kernel_one, bias_one, kernel_two, bias_two), 'member')...]
  transfers between devices with their start and end apart: 17 -> 18, of which waited for: 1 -> 1; matrix products, arithmetic and copies ran while one was open for 7% -> 2% of each run, Pallas kernels for 0% -> 0%
where the time goes in v1:
time: 1780 us; the launch traced here: 1750 us
  waiting for transfers between devices  1280 us (72%)
  blocking collectives  320 us (18%)
  local copies, waits for them, and re-layouts  56.4 us (3%)
  starting transfers between devices  41.2 us (2%)
  other arithmetic  18.3 us (1%)
    psum x1, waiting for transfers between devices, per_device(): lax.psum(lax.psum((kernel_one, bias_one, kernel_two, bias_two), 'member')...  1280 us
    psum x1, blocking collectives, per_device(): lax.psum(lax.psum((kernel_one, bias_one, kernel_two, bias_two), 'member')...  315 us
    ppermute x16, starting transfers between devices, shifted(): return lax.ppermute(value, axis, pairs)  41.1 us
  transfers between devices with their start and end apart: 18, of which 1 were waited for; matrix products, arithmetic and copies ran while one was open for 2% of the time, Pallas kernels for 0%

profile of v1, /device:TPU:2, one launch (start us, length us, event | category | flops | bytes accessed | tf_op | source)
XLA Modules:
  0.0 1750.4 jit_solution(9610941367719698346)
XLA Ops:
  7.2 0.8 slice_bitcast_fusion.27
  8.0 1.0 fusion.81
  10.2 1.6 collective-permute-start.3
  11.8 3.5 collective-permute-start.2
  15.3 6.0 collective-permute-start.1
  22.9 1.2 copy.158
  24.8 1.2 copy.140
  27.6 1.1 fusion.79
  29.2 1.1 constant_dynamic-update-slice_fusion.5
  30.4 1.1 constant_dynamic-update-slice_fusion.3
  31.5 1.5 fusion.78
  33.5 1.4 fusion.84
  36.3 3.8 collective-permute-start.6
  40.0 6.2 collective-permute-start.5
  46.2 1.9 constant_dynamic-update-slice_fusion.18
  48.1 0.9 constant_dynamic-update-slice_fusion.17
  49.1 0.9 constant_dynamic-update-slice_fusion.16
  50.0 1.9 constant_dynamic-update-slice_fusion.15
  51.9 0.9 constant_dynamic-update-slice_fusion.14
  52.8 0.9 constant_dynamic-update-slice_fusion.13
  53.6 0.9 constant_dynamic-update-slice_fusion.12
  54.5 0.9 constant_dynamic-update-slice_fusion.11
  55.5 0.9 constant_dynamic-update-slice_fusion.10
  56.3 6.7 copy.180
  64.6 0.8 constant_dynamic-update-slice_fusion.9
  66.4 4.8 copy.182
  71.2 2.5 convert_reduce_fusion
  76.5 2.3 fusion.2
  80.7 6.7 copy.183
  88.2 0.8 copy.260
  93.7 1.4 select_select_fusion.3
  95.1 0.9 rev.35
  96.0 0.9 select_convert_fusion.1
  97.1 3.8 collective-permute-start.10
  100.8 6.0 collective-permute-start.9
  106.8 4.5 fusion.86
  111.5 1.1 copy.185
  113.7 0.9 convert_reduce_fusion.1
  117.4 2.1 fusion
  120.1 4.5 fusion.85
  125.0 3.8 collective-permute-start.14
  128.8 6.0 collective-permute-start.13
  134.8 5.1 all-reduce.4
  139.9 315.2 %all-reduce.2 = (f32[128]{0:T(128)S(1)}, f32[128]{0:T(128)S(1)}) all-reduce(f32[128]{0:T(128)S(1)} %get-tuple-element.316, f32[128]{0:T(128)S(1)} %get-tuple-element.317), channel_id=1, replica_groups=mesh['tile'=128,'member'=2] {'tile'}, use_global_device_ids=true, to_apply=%region_5.6 | all-reduce | flops 256 | bytes 2048 | tf_op jit(solution)/shard_map/psum | solution.py:212
  457.4 1.1 copy.186
  458.5 1280.8 %all-reduce.9.cloned.1.call-done = (f32[3,3,128,128]{3,2,1,0:T(8,128)}, f32[3,3,128,128]{3,2,1,0:T(8,128)}) async-done(((f32[3,3,128,128]{3,2,1,0:T(8,128)}, f32[3,3,128,128]{3,2,1,0:T(8,128)}), (f32[3,3,128,128]{3,2,1,0:T(8,128)}, f32[3,3,128,128]{3,2,1,0:T(8,128)})) %all-reduce.9.cloned.1.call-update) | async-done | bytes 1179664 | tf_op jit(solution)/shard_map/psum | solution.py:212
  1739.3 1.9 broadcast_multiply_fusion.1
  1741.3 1.9 broadcast_multiply_fusion
  (261 shorter events, 26.4 us)
Async XLA Ops:
  7.2 20.0 %copy-start = (bf16[1,1,2,32,32,128]{5,4,3,2,1,0:T(8,128)(2,1)S(1)}, bf16[1,1,2,32,32,128]{5,4,3,2,1,0:T(8,128)(2,1)}, u32[]{:S(2)}) copy-start(bf16[1,1,2,32,32,128]{5,4,3,2,1,0:T(8,128)(2,1)} %param.55) | copy-start | bytes 1572868
  7.2 449.5 %all-reduce.11.cloned.1.call-start = ((), (), s32[]{:S(2)}) async-start(), calls=%async_computation.1 | async-start | bytes 2359296 | tf_op jit(solution)/shard_map/psum | solution.py:213
  9.8 26.1 %copy-start.22 = (pred[4]{0:T(512)(128)(4,1)}, pred[4]{0:T(512)(128)(4,1)S(1)}, u32[]{:S(2)}) copy-start(pred[4]{0:T(512)(128)(4,1)S(1)} %get-tuple-element.431) | copy-start | bytes 16
  9.8 26.1 %copy-start.24 = (pred[4]{0:T(512)(128)(4,1)}, pred[4]{0:T(512)(128)(4,1)S(1)}, u32[]{:S(2)}) copy-start(pred[4]{0:T(512)(128)(4,1)S(1)} %get-tuple-element.432) | copy-start | bytes 16
  9.8 26.1 %copy-start.26 = (pred[4]{0:T(512)(128)(4,1)}, pred[4]{0:T(512)(128)(4,1)S(1)}, u32[]{:S(2)}) copy-start(pred[4]{0:T(512)(128)(4,1)S(1)} %get-tuple-element.433) | copy-start | bytes 16
  9.8 26.1 %copy-start.28 = (pred[4]{0:T(512)(128)(4,1)}, pred[4]{0:T(512)(128)(4,1)S(1)}, u32[]{:S(2)}) copy-start(pred[4]{0:T(512)(128)(4,1)S(1)} %get-tuple-element.434) | copy-start | bytes 16
  9.8 26.1 %copy-start.32 = (pred[4]{0:T(512)(128)(4,1)}, pred[4]{0:T(512)(128)(4,1)S(1)}, u32[]{:S(2)}) copy-start(pred[4]{0:T(512)(128)(4,1)S(1)} %get-tuple-element.430) | copy-start | bytes 16
  10.1 16.6 collective-permute-start
  10.2 16.5 collective-permute-start.3
  11.8 15.0 collective-permute-start.2
  15.3 11.5 collective-permute-start.1
  22.8 40.4 %copy-start.14 = (pred[4]{0:T(512)(128)(4,1)}, pred[4]{0:T(512)(128)(4,1)S(1)}, u32[]{:S(2)}) copy-start(pred[4]{0:T(512)(128)(4,1)S(1)} %get-tuple-element.436) | copy-start | bytes 16
  22.8 40.4 %copy-start.16 = (pred[4]{0:T(512)(128)(4,1)}, pred[4]{0:T(512)(128)(4,1)S(1)}, u32[]{:S(2)}) copy-start(pred[4]{0:T(512)(128)(4,1)S(1)} %get-tuple-element.437) | copy-start | bytes 16
  22.9 40.4 %copy-start.18 = (pred[4]{0:T(512)(128)(4,1)}, pred[4]{0:T(512)(128)(4,1)S(1)}, u32[]{:S(2)}) copy-start(pred[4]{0:T(512)(128)(4,1)S(1)} %get-tuple-element.438) | copy-start | bytes 16
  22.9 40.4 %copy-start.20 = (pred[4]{0:T(512)(128)(4,1)}, pred[4]{0:T(512)(128)(4,1)S(1)}, u32[]{:S(2)}) copy-start(pred[4]{0:T(512)(128)(4,1)S(1)} %get-tuple-element.439) | copy-start | bytes 16
  22.9 40.4 %copy-start.30 = (pred[4]{0:T(512)(128)(4,1)}, pred[4]{0:T(512)(128)(4,1)S(1)}, u32[]{:S(2)}) copy-start(pred[4]{0:T(512)(128)(4,1)S(1)} %get-tuple-element.435) | copy-start | bytes 16
  29.2 4.3 copy-start.5
  35.9 16.8 copy-start.2
  36.0 17.7 %copy-start.4 = (bf16[2,32,32,128]{3,2,1,0:T(8,128)(2,1)S(1)}, bf16[2,32,32,128]{3,2,1,0:T(8,128)(2,1)}, u32[]{:S(2)}) copy-start(bf16[2,32,32,128]{3,2,1,0:T(8,128)(2,1)} %get-tuple-element.357) | copy-start | bytes 1572868
  36.0 18.5 %copy-start.3 = (bf16[2,32,32,128]{3,2,1,0:T(8,128)(2,1)S(1)}, bf16[2,32,32,128]{3,2,1,0:T(8,128)(2,1)}, u32[]{:S(2)}) copy-start(bf16[2,32,32,128]{3,2,1,0:T(8,128)(2,1)} %get-tuple-element.356) | copy-start | bytes 1572868
  36.0 19.5 %copy-start.1 = (bf16[2,32,32,128]{3,2,1,0:T(8,128)(2,1)S(1)}, bf16[2,32,32,128]{3,2,1,0:T(8,128)(2,1)}, u32[]{:S(2)}) copy-start(bf16[2,32,32,128]{3,2,1,0:T(8,128)(2,1)} %get-tuple-element.354) | copy-start | bytes 1572868
  36.1 27.0 %collective-permute-start.4 = (bf16[2,32,128]{2,1,0:T(8,128)(2,1)S(1)}, bf16[2,32,128]{2,1,0:T(8,128)(2,1)S(1)}, u32[]{:S(2)}, u32[]{:S(2)}) collective-permute-start(bf16[2,32,128]{2,1,0:T(8,128)(2,1)S(1)} %get-tuple-element.392), channel_id=1, source_target_pairs={{0,2},{2,4},{4,6},{6,8},{8,10},{10,12},{12,14},{14,16},{16,18},{18... | collective-permute-start | bytes 49160 | tf_op jit(solution)/shard_map/ppermute | solution.py:14
  36.2 26.9 %collective-permute-start.7 = (bf16[2,32,128]{2,1,0:T(8,128)(2,1)S(1)}, bf16[2,32,128]{2,1,0:T(8,128)(2,1)S(1)}, u32[]{:S(2)}, u32[]{:S(2)}) collective-permute-start(bf16[2,32,128]{2,1,0:T(8,128)(2,1)S(1)} %get-tuple-element.393), channel_id=1, source_target_pairs={{0,16},{2,18},{4,20},{6,22},{8,24},{10,26},{12,28},{14,30},{16,32}... | collective-permute-start | bytes 49160 | tf_op jit(solution)/shard_map/ppermute | solution.py:14
  36.3 26.8 %collective-permute-start.6 = (bf16[2,32,128]{2,1,0:T(8,128)(2,1)S(1)}, bf16[2,32,128]{2,1,0:T(8,128)(2,1)S(1)}, u32[]{:S(2)}, u32[]{:S(2)}) collective-permute-start(bf16[2,32,128]{2,1,0:T(8,128)(2,1)S(1)} %get-tuple-element.394), channel_id=1, source_target_pairs={{0,254},{2,0},{4,2},{6,4},{8,6},{10,8},{12,10},{14,12},{16,14},{18... | collective-permute-start | bytes 49160 | tf_op jit(solution)/shard_map/ppermute | solution.py:14
  40.0 23.0 %collective-permute-start.5 = (bf16[2,32,128]{2,1,0:T(8,128)(2,1)S(1)}, bf16[2,32,128]{2,1,0:T(8,128)(2,1)S(1)}, u32[]{:S(2)}, u32[]{:S(2)}) collective-permute-start(bf16[2,32,128]{2,1,0:T(8,128)(2,1)S(1)} %get-tuple-element.395), channel_id=1, source_target_pairs={{0,240},{2,242},{4,244},{6,246},{8,248},{10,250},{12,252},{14,254}... | collective-permute-start | bytes 49160 | tf_op jit(solution)/shard_map/ppermute | solution.py:14
  66.4 4.9 copy-start.6
  66.4 4.9 copy-start.38
  66.4 4.9 copy-start.39
  96.9 15.9 collective-permute-start.8
  97.0 15.8 collective-permute-start.11
  97.1 15.8 collective-permute-start.10
  100.8 12.0 collective-permute-start.9
  106.8 6.0 copy-start.15
  106.8 6.1 copy-start.17
  106.8 6.1 copy-start.19
  106.8 6.1 copy-start.21
  106.8 6.2 copy-start.31
  117.4 2.6 copy-start.23
  117.4 2.6 copy-start.25
  117.4 2.6 copy-start.27
  117.4 2.6 copy-start.29
  119.5 5.2 copy-start.33
  119.5 15.2 copy-start.40
  124.7 1614.7 %all-reduce.9.cloned.1.call-start = ((), (), s32[]{:S(2)}) async-start(), calls=%async_computation | async-start | bytes 2359296 | tf_op jit(solution)/shard_map/psum | solution.py:212
  124.9 331.5 %collective-permute-start.12 = (bf16[2,32,128]{2,1,0:T(8,128)(2,1)S(1)}, bf16[2,32,128]{2,1,0:T(8,128)(2,1)S(1)}, u32[]{:S(2)}, u32[]{:S(2)}) collective-permute-start(bf16[2,32,128]{2,1,0:T(8,128)(2,1)S(1)} %get-tuple-element.378), channel_id=1, source_target_pairs={{0,2},{2,4},{4,6},{6,8},{8,10},{10,12},{12,14},{14,16},{16,18},{18... | collective-permute-start | bytes 49160 | tf_op jit(solution)/shard_map/ppermute | solution.py:14
  124.9 331.4 %collective-permute-start.15 = (bf16[2,32,128]{2,1,0:T(8,128)(2,1)S(1)}, bf16[2,32,128]{2,1,0:T(8,128)(2,1)S(1)}, u32[]{:S(2)}, u32[]{:S(2)}) collective-permute-start(bf16[2,32,128]{2,1,0:T(8,128)(2,1)S(1)} %get-tuple-element.379), channel_id=1, source_target_pairs={{0,16},{2,18},{4,20},{6,22},{8,24},{10,26},{12,28},{14,30},{16,32}... | collective-permute-start | bytes 49160 | tf_op jit(solution)/shard_map/ppermute | solution.py:14
  125.0 331.3 %collective-permute-start.14 = (bf16[2,32,128]{2,1,0:T(8,128)(2,1)S(1)}, bf16[2,32,128]{2,1,0:T(8,128)(2,1)S(1)}, u32[]{:S(2)}, u32[]{:S(2)}) collective-permute-start(bf16[2,32,128]{2,1,0:T(8,128)(2,1)S(1)} %get-tuple-element.380), channel_id=1, source_target_pairs={{0,254},{2,0},{4,2},{6,4},{8,6},{10,8},{12,10},{14,12},{16,14},{18... | collective-permute-start | bytes 49160 | tf_op jit(solution)/shard_map/ppermute | solution.py:14
  128.8 327.6 %collective-permute-start.13 = (bf16[2,32,128]{2,1,0:T(8,128)(2,1)S(1)}, bf16[2,32,128]{2,1,0:T(8,128)(2,1)S(1)}, u32[]{:S(2)}, u32[]{:S(2)}) collective-permute-start(bf16[2,32,128]{2,1,0:T(8,128)(2,1)S(1)} %get-tuple-element.381), channel_id=1, source_target_pairs={{0,240},{2,242},{4,244},{6,246},{8,248},{10,250},{12,252},{14,254}... | collective-permute-start | bytes 49160 | tf_op jit(solution)/shard_map/ppermute | solution.py:14
  (11 other events, 17.5 us)
Sparse Core Ops, SparseCore 0:
  124.8 51.7 all-reduce.10
  456.8 1282.4 all-reduce.8
